TPU v7x, 512 devices: a whole 4x8x8 slice. The times are simulated.
512 devices in a mesh: pb: 32 (over z, x), ka: 16 (over y, core).
Axes of the slice: x: 4, y: 8, z: 8, core: 2. Of those that a mesh axis runs over, the one named last changes fastest.
Arguments:
- features: bfloat16 [65536, 1024], P(('pb', 'ka')), may hold values from -8.5 to 8.5
- order: int32 [65536], P(('pb', 'ka')), may hold values from 0 to 127, as said below
- neighbours: int32 [512, 24], P('pb'), may hold values from 0 to 511, as said below
- counts: int32 [512], P('pb'), may hold values from 1 to 24, as said below
- qkv_weight: bfloat16 [1024, 1536], P(('pb', 'ka')), may hold values from -0.25 to 0.25
- out_weight: bfloat16 [512, 1024], P(None, ('pb', 'ka')), may hold values from -1 to 1
Outputs:
- mixed: bfloat16 [65536, 1024], P(('pb', 'ka'))
Inputs may be any that keep to these rules, and one draw needn't show every extreme that they name: `order`: each aligned group of 128 entries is a permutation of 0 to 127. `neighbours`: entry 0 of the list of block a is a itself; the first counts[a] entries are distinct and lie in a's slab of 16 blocks or in the slabs just before and after it, cyclically; slots from counts[a] on hold some block id and are not part of the list. `counts`: some block's list fills all 24 slots.
All inputs are finite; a program needn't handle non-finite values.
Results may differ from a plain program's by a relative error of at most 0.012.
The roundings to bfloat16 on the way count: a program that leaves them out, or rounds other values in their place, can miss the bound.
Values may be sent and summed in bfloat16 or wider, within the bound.
No kernel may reach another device: no remote copies, remote signals or barrier semaphores. Data moves between devices by JAX's collectives and lax.ppermute only.
A program may use at most 64 MiB of HBM per device.

v0:
```python
import jax
import jax.numpy as jnp
from jax import lax
from jax.sharding import PartitionSpec as P

HD = 64
BLK = 128


def padded(array, sides, width):
    for axis, dim in sides:
        size, length = (lax.axis_size(axis), array.shape[dim])
        up = [(i, (i + 1) % size) for i in range(size)]
        down = [(j, i) for i, j in up]
        last = lax.slice_in_dim(array, length - width, length, axis=dim)
        leading = lax.slice_in_dim(array, 0, width, axis=dim)
        before = lax.ppermute(last, axis, up)
        after = lax.ppermute(leading, axis, down)
        array = jnp.concatenate([before, array, after], axis=dim)
    return array


def attend_rows(query_rows, allow_rows, near_keys, near_values, score_scale):
    row_total = query_rows.shape[0]
    head_count = query_rows.shape[1]
    attn_width = head_count * query_rows.shape[2]
    tile_rows = 512
    tile_count = row_total // tile_rows

    def attend(tile_args):
        query_tile, allow_tile = tile_args
        allowed = jnp.repeat(allow_tile, BLK, axis=1)
        scores = (
            jnp.einsum("qhd,khd->hqk", query_tile, near_keys, preferred_element_type=jnp.float32)
            * score_scale
        )
        row_max = jnp.max(jnp.where(allowed[None], scores, -1e30), axis=-1)
        row_shift = row_max.astype(jnp.bfloat16)
        soft_weights = jnp.where(
            allowed[None], jnp.exp(scores - row_shift.astype(jnp.float32)[..., None]), 0.0
        )
        group_total = jnp.sum(soft_weights, axis=-1).T
        numerator = jnp.einsum(
            "hqk,khd->qhd",
            soft_weights.astype(jnp.bfloat16),
            near_values,
            preferred_element_type=jnp.float32,
        )
        positive = group_total > 0
        partial_value = jnp.where(
            positive[..., None], numerator / jnp.where(positive, group_total, 1.0)[..., None], 0.0
        )
        return (
            partial_value.astype(jnp.bfloat16).reshape(tile_rows, attn_width),
            row_shift.T,
            group_total.astype(jnp.bfloat16),
        )

    tiled = lax.map(
        attend,
        (
            query_rows.reshape(tile_count, tile_rows, head_count, query_rows.shape[2]),
            allow_rows.reshape(tile_count, tile_rows, -1),
        ),
    )
    return (
        tiled[0].reshape(row_total, attn_width),
        tiled[1].reshape(row_total, head_count),
        tiled[2].reshape(row_total, head_count),
    )


def body(features, order, neighbours, counts, qkv_weight, out_weight):
    dev_rows = features.shape[0]
    sorted_rows = jnp.take(features, order, axis=0)
    attn_width = qkv_weight.shape[1] // 3
    head_count = attn_width // HD
    score_scale = HD ** (-0.5)
    projected = jnp.dot(
        sorted_rows,
        lax.all_gather(qkv_weight, ("pb", "ka"), axis=0, tiled=True),
        preferred_element_type=jnp.float32,
    )
    own_queries = projected[:, :attn_width].astype(jnp.bfloat16)
    keys_values = projected[:, attn_width:].astype(jnp.bfloat16)
    near = padded(keys_values, (("pb", 0),), dev_rows)
    slab_index = lax.axis_index("pb")
    group_index = lax.axis_index("ka")
    slab_count = lax.axis_size("pb")
    group_count = lax.axis_size("ka")
    dev_blocks = dev_rows // BLK
    slab_of = (slab_index + jnp.arange(3) - 1) % slab_count
    listed_slot = jnp.arange(neighbours.shape[1])[None, :] < counts[:, None]
    slab_queries = lax.all_gather(own_queries, "ka", axis=0, tiled=True)
    near_keys = near[:, :attn_width].reshape(3 * dev_rows, head_count, HD)
    near_values = near[:, attn_width:].reshape(3 * dev_rows, head_count, HD)
    block_ids = (
        (slab_of[:, None] * group_count + group_index) * dev_blocks
        + jnp.arange(dev_blocks)[None, :]
    ).reshape(-1)
    member = jnp.any(
        (neighbours[:, :, None] == block_ids[None, None, :]) & listed_slot[:, :, None], axis=1
    )
    row_member = jnp.repeat(member, BLK, axis=0)
    partial_value, row_shift, group_total = attend_rows(
        slab_queries.reshape(-1, head_count, HD), row_member, near_keys, near_values, score_scale
    )
    received = (
        lax.all_to_all(partial_value[None], "ka", split_axis=1, concat_axis=0, tiled=True),
        lax.all_to_all(row_shift[None], "ka", split_axis=1, concat_axis=0, tiled=True),
        lax.all_to_all(group_total[None], "ka", split_axis=1, concat_axis=0, tiled=True),
    )
    group_out = received[0].reshape(group_count, dev_rows, head_count, HD).astype(jnp.float32)
    group_max = received[1].astype(jnp.float32)
    total_rounded = received[2].astype(jnp.float32)
    top_shift = jnp.max(group_max, axis=0, keepdims=True)
    weight_g = total_rounded * jnp.exp(group_max - top_shift)
    combined = (
        jnp.sum(weight_g[..., None] * group_out, axis=0) / jnp.sum(weight_g, axis=0)[..., None]
    )
    attended = combined.reshape(dev_rows, attn_width).astype(jnp.bfloat16)
    mixed = jnp.dot(
        attended,
        lax.all_gather(out_weight, ("pb", "ka"), axis=1, tiled=True),
        preferred_element_type=jnp.float32,
    )
    return mixed.astype(jnp.bfloat16)


def solution(mesh):
    return jax.shard_map(
        body,
        mesh=mesh,
        in_specs=(
            P(("pb", "ka"), None),
            P(("pb", "ka")),
            P("pb", None),
            P("pb"),
            P(("pb", "ka"), None),
            P(None, ("pb", "ka")),
        ),
        out_specs=P(("pb", "ka"), None),
        check_vma=False,
    )
```

profile of v0, /device:TPU:1, one launch (start us, length us, event | category | flops | bytes accessed | tf_op | source)
XLA Modules:
  0.0 470.9 jit_solution(14192227212871008691)
XLA Ops:
  10.2 124.0 %all-gather.8.cloned.1.call-done = bf16[512,2,1536]{2,1,0:T(2,128)(2,1)} async-done(((bf16[1,2,1536]{2,1,0:T(2,128)(2,1)}), bf16[512,2,1536]{2,1,0:T(2,128)(2,1)}) %all-gather.8.cloned.1.call-update) | async-done | bytes 3145744 | tf_op jit(solution)/shard_map/all_gather | solution.py:81
  134.2 6.3 %reshape.136 = bf16[1024,1536]{1,0:T(8,128)(2,1)S(1)} reshape(bf16[512,2,1536]{2,1,0:T(2,128)(2,1)} %all-gather.8.cloned.1.call-done) | data formatting | bytes 6291456
  144.6 3.1 collective-permute-start
  147.6 5.7 %collective-permute-start.1 = (bf16[128,1024]{1,0:T(8,128)(2,1)S(1)}, bf16[128,1024]{1,0:T(8,128)(2,1)S(1)}, u32[]{:S(2)}, u32[]{:S(2)}) collective-permute-start(bf16[128,1024]{1,0:T(8,128)(2,1)S(1)} %slice.21), channel_id=1, source_target_pairs={{16,0},{32,16},{48,32},{64,48},{80,64},{96,80},{112,96},{128,112},... | collective-permute-start | bytes 786440 | tf_op jit(solution)/shard_map/ppermute | solution.py:18
  153.8 3.6 collective-permute-done
  158.8 22.9 %all-gather.6.cloned.1.call-done = bf16[2048,512]{1,0:T(8,128)(2,1)} async-done(((bf16[128,512]{1,0:T(8,128)(2,1)}), bf16[2048,512]{1,0:T(8,128)(2,1)}) %all-gather.6.cloned.1.call-update) | async-done | bytes 2097168 | tf_op jit(solution)/shard_map/all_gather | solution.py:94
  181.7 6.2 %reshape.139 = bf16[4,512,8,64]{3,2,1,0:T(8,128)(2,1)} reshape(bf16[2048,512]{1,0:T(8,128)(2,1)} %all-gather.6.cloned.1.call-done) | data formatting | bytes 4194304 | tf_op jit(solution)/shard_map/reshape;reshape | solution.py:62
  187.9 5.5 %copy.79 = bf16[4,512,8,64]{1,3,2,0:T(8,128)(2,1)} copy(bf16[4,512,8,64]{3,2,1,0:T(8,128)(2,1)} %reshape.139) | data formatting | bytes 4194304 | tf_op jit(solution)/shard_map/while | solution.py:59
  193.3 24.9 %while.14 = (s32[]{:T(128)}, bf16[4,512,512]{2,1,0:T(8,128)(2,1)}, bf16[4,512,8]{1,2,0:T(8,128)(2,1)S(1)}, bf16[4,512,8]{1,2,0:T(8,128)(2,1)S(1)}, pred[4,512,3]...) while((s32[]{:T(128)}, bf16[4,512,512]{2,1,0:T(8,128)(2,1)}, ...), condition=%wide.region_4.5_spmd, body=%wide.region_1.4_spmd.sunk | while | flops 420753408 | bytes 23795300 | solution.py:59
  219.4 12.2 %reduce.6 = bf16[2048,8]{1,0:T(8,128)(2,1)} reduce(bf16[2048,1,8]{2,1,0:T(2,128)(2,1)S(1)} %bitcast.101, bf16[]{:T(256)} %broadcast.127), dimensions={1}, to_apply=%bitcast.57.reduce_sub_computation | reduce | bytes 65538
  233.8 4.9 %all-to-all-start.1 = ((bf16[16,2,512]{2,1,0:T(2,128)(2,1)}), bf16[16,2,512]{2,1,0:T(2,128)(2,1)S(1)}, u32[]{:S(2)}, u32[]{:S(2)}) async-start(bf16[16,2,512]{2,1,0:T(2,128)(2,1)} %reshape.144), calls=%async_computation.1 | async-start | bytes 65536 | tf_op jit(solution)/shard_map/all_to_all | solution.py:110
  239.5 12.2 %reduce.7 = bf16[2048,8]{1,0:T(8,128)(2,1)} reduce(bf16[2048,1,8]{2,1,0:T(2,128)(2,1)S(1)} %bitcast.102, bf16[]{:T(256)} %broadcast.127), dimensions={1}, to_apply=%bitcast.55.reduce_sub_computation | reduce | bytes 65538
  253.9 7.2 %all-to-all-start = ((bf16[16,2,512]{2,1,0:T(2,128)(2,1)}), bf16[16,2,512]{2,1,0:T(2,128)(2,1)S(1)}, u32[]{:S(2)}, u32[]{:S(2)}) async-start(bf16[16,2,512]{2,1,0:T(2,128)(2,1)} %reshape.142), calls=%async_computation | async-start | bytes 65536 | tf_op jit(solution)/shard_map/all_to_all | solution.py:111
  261.1 18.5 %copy.97 = bf16[1,2048,512]{2,0,1:T(2,128)(2,1)} copy(bf16[1,2048,512]{2,1,0:T(8,128)(2,1)S(1)} %bitcast.105) | data formatting | bytes 4194304 | tf_op jit(solution)/shard_map/broadcast_in_dim;reshape | solution.py:109
  279.7 14.0 %reduce.5 = bf16[2048,512]{1,0:T(8,128)(2,1)S(1)} reduce(bf16[2048,1,512]{2,1,0:T(2,128)(2,1)} %bitcast.95, bf16[]{:T(256)} %broadcast.127), dimensions={1}, to_apply=%bitcast.69.reduce_sub_computation | reduce | bytes 4194306
  293.7 2.8 reshape.140
  296.5 7.2 %all-to-all-start.2 = ((bf16[16,2,32768]{2,1,0:T(2,128)(2,1)}), bf16[16,2,32768]{2,1,0:T(2,128)(2,1)S(1)}, u32[]{:S(2)}, u32[]{:S(2)}) async-start(bf16[16,2,32768]{2,1,0:T(2,128)(2,1)} %reshape.140), calls=%async_computation.2 | async-start | bytes 4194304 | tf_op jit(solution)/shard_map/all_to_all | solution.py:109
  304.4 126.7 %all-gather.10.cloned.1.call-done = bf16[512,2,512]{2,1,0:T(2,128)(2,1)} async-done(((bf16[1,2,512]{2,1,0:T(2,128)(2,1)}), bf16[512,2,512]{2,1,0:T(2,128)(2,1)}) %all-gather.10.cloned.1.call-update) | async-done | bytes 1048592 | tf_op jit(solution)/shard_map/all_gather | solution.py:124
  432.6 2.5 reshape.145
  437.4 2.5 reshape.143
  442.2 6.8 %reshape.141 = bf16[2048,1,512]{2,1,0:T(2,128)(2,1)} reshape(bf16[16,2,32768]{2,1,0:T(2,128)(2,1)S(1)} %all-to-all-done.2) | data formatting | bytes 4194304
  449.0 4.6 copy_convert_fusion
  453.6 5.5 %copy.88 = f32[1,2048,512]{1,2,0:T(8,128)} copy(f32[1,2048,512]{2,1,0:T(8,128)} %copy_convert_fusion) | data formatting | bytes 8388608 | tf_op jit(solution)/shard_map/convert_element_type | solution.py:113
  459.1 3.1 copy.94
  (99 shorter events, 49.2 us)
Async XLA Ops:
  6.5 1.4 copy-start
  6.5 127.7 %all-gather.8.cloned.1.call-start = ((), (), s32[]{:S(2)}) async-start(), calls=%async_computation.4 | async-start | bytes 3151872 | tf_op jit(solution)/shard_map/all_gather | solution.py:81
  7.3 174.4 %all-gather.6.cloned.1.call-start = ((), (), s32[]{:S(2)}) async-start(), calls=%async_computation.3 | async-start | bytes 2228224 | tf_op jit(solution)/shard_map/all_gather | solution.py:94
  10.2 143.2 %copy-start.4 = (s32[16]{0:T(128)S(1)}, s32[16]{0:T(128)}, u32[]{:S(2)}) copy-start(s32[16]{0:T(128)} %param.11) | copy-start | bytes 196
  10.2 143.3 %copy-start.3 = (s32[16,24]{1,0:T(8,128)S(1)}, s32[16,24]{1,0:T(8,128)}, u32[]{:S(2)}) copy-start(s32[16,24]{1,0:T(8,128)} %param.10) | copy-start | bytes 4612
  142.2 0.7 copy-start.2
  144.6 12.8 %collective-permute-start = (bf16[128,1024]{1,0:T(8,128)(2,1)S(1)}, bf16[128,1024]{1,0:T(8,128)(2,1)S(1)}, u32[]{:S(2)}, u32[]{:S(2)}) collective-permute-start(bf16[128,1024]{1,0:T(8,128)(2,1)S(1)} %slice.21), channel_id=1, source_target_pairs={{0,16},{16,32},{32,48},{48,64},{64,80},{80,96},{96,112},{112,128},... | collective-permute-start | bytes 786440 | tf_op jit(solution)/shard_map/ppermute | solution.py:17
  147.6 10.6 %collective-permute-start.1 = (bf16[128,1024]{1,0:T(8,128)(2,1)S(1)}, bf16[128,1024]{1,0:T(8,128)(2,1)S(1)}, u32[]{:S(2)}, u32[]{:S(2)}) collective-permute-start(bf16[128,1024]{1,0:T(8,128)(2,1)S(1)} %slice.21), channel_id=1, source_target_pairs={{16,0},{32,16},{48,32},{64,48},{80,64},{96,80},{112,96},{128,112},... | collective-permute-start | bytes 786440 | tf_op jit(solution)/shard_map/ppermute | solution.py:18
  218.2 42.9 %copy-start.1 = (bf16[4,512,512]{2,1,0:T(8,128)(2,1)S(1)}, bf16[4,512,512]{2,1,0:T(8,128)(2,1)}, u32[]{:S(2)}) copy-start(bf16[4,512,512]{2,1,0:T(8,128)(2,1)} %get-tuple-element.51) | copy-start | bytes 6291460
  233.8 20.1 %all-to-all-start.1 = ((bf16[16,2,512]{2,1,0:T(2,128)(2,1)}), bf16[16,2,512]{2,1,0:T(2,128)(2,1)S(1)}, u32[]{:S(2)}, u32[]{:S(2)}) async-start(bf16[16,2,512]{2,1,0:T(2,128)(2,1)} %reshape.144), calls=%async_computation.1 | async-start | bytes 65536 | tf_op jit(solution)/shard_map/all_to_all | solution.py:110
  253.9 42.6 %all-to-all-start = ((bf16[16,2,512]{2,1,0:T(2,128)(2,1)}), bf16[16,2,512]{2,1,0:T(2,128)(2,1)S(1)}, u32[]{:S(2)}, u32[]{:S(2)}) async-start(bf16[16,2,512]{2,1,0:T(2,128)(2,1)} %reshape.142), calls=%async_computation | async-start | bytes 65536 | tf_op jit(solution)/shard_map/all_to_all | solution.py:111
  296.5 145.7 %all-to-all-start.2 = ((bf16[16,2,32768]{2,1,0:T(2,128)(2,1)}), bf16[16,2,32768]{2,1,0:T(2,128)(2,1)S(1)}, u32[]{:S(2)}, u32[]{:S(2)}) async-start(bf16[16,2,32768]{2,1,0:T(2,128)(2,1)} %reshape.140), calls=%async_computation.2 | async-start | bytes 4194304 | tf_op jit(solution)/shard_map/all_to_all | solution.py:109
  303.7 127.5 %all-gather.10.cloned.1.call-start = ((), (), s32[]{:S(2)}) async-start(), calls=%async_computation.5 | async-start | bytes 1050624 | tf_op jit(solution)/shard_map/all_gather | solution.py:124
Sparse Core Ops, SparseCore 0:
  11.5 122.6 all-gather.7
  143.7 37.9 all-gather.5
  308.7 122.4 all-gather.9
where the time goes:
time: 472 us; the launch traced here: 471 us
  waiting for transfers between devices  279 us (59%)
  local copies, waits for them, and re-layouts  80.9 us (17%)
  other arithmetic  51.1 us (11%)
  starting transfers between devices  28.5 us (6%)
  matrix products  17.6 us (4%)
  between operations  13.3 us (3%)
    all_gather x1, waiting for transfers between devices, body(): lax.all_gather(out_weight, ('pb', 'ka'), axis=1, tiled=True)  127 us
    all_gather x1, waiting for transfers between devices, body(): lax.all_gather(qkv_weight, ('pb', 'ka'), axis=0, tiled=True)  124 us
    unnamed x3, other arithmetic  38.5 us
    unnamed x20, local copies, waits for them, and re-layouts  31.1 us
    all_gather x1, waiting for transfers between devices, body(): slab_queries = lax.all_gather(own_queries, 'ka', axis=0, tiled=True)  22.9 us
    another operation x1, local copies, waits for them, and re-layouts, body(): partial_value[None]  18.5 us
  transfers between devices with their start and end apart: 8, of which 5 were waited for; matrix products, arithmetic and copies ran while one was open for 14% of the time, Pallas kernels for 0%

commit v1 on v0

--- a/solution.py
+++ b/solution.py
@@ -5,6 +5,14 @@
 
 HD = 64
 BLK = 128
+
+
+def gather_from_all(shard, axis, dim):
+    size = lax.axis_size(axis)
+    repeats = [size if d == dim else 1 for d in range(shard.ndim)]
+    return lax.all_to_all(
+        jnp.tile(shard, repeats), axis, split_axis=dim, concat_axis=dim, tiled=True
+    )
 
 
 def padded(array, sides, width):
@@ -91,7 +99,7 @@
     dev_blocks = dev_rows // BLK
     slab_of = (slab_index + jnp.arange(3) - 1) % slab_count
     listed_slot = jnp.arange(neighbours.shape[1])[None, :] < counts[:, None]
-    slab_queries = lax.all_gather(own_queries, "ka", axis=0, tiled=True)
+    slab_queries = gather_from_all(own_queries, "ka", 0)
     near_keys = near[:, :attn_width].reshape(3 * dev_rows, head_count, HD)
     near_values = near[:, attn_width:].reshape(3 * dev_rows, head_count, HD)
     block_ids = (

time: 472 us -> 489 us (1.036)
  waiting for transfers between devices: 279 us -> 289 us
    all_to_all x0 -> x1, waiting for transfers between devices: none -> 32 us  [gather_from_all(): lax.all_to_all(jnp.tile(shard, repeats), axis, split_axis=dim, concat_axi...]
    all_gather x1 -> x0, waiting for transfers between devices: 22.9 us -> none  [body(): slab_queries = lax.all_gather(own_queries, 'ka', axis=0, tiled=True)]
    unnamed x20 -> x22, local copies, waits for them, and re-layouts: 31.1 us -> 31.1 us
where the time goes in v1:
time: 489 us; the launch traced here: 488 us
  waiting for transfers between devices  289 us (59%)
  local copies, waits for them, and re-layouts  79.3 us (16%)
  other arithmetic  51.1 us (10%)
  starting transfers between devices  32.5 us (7%)
  matrix products  21.8 us (4%)
  between operations  13.6 us (3%)
    all_gather x1, waiting for transfers between devices, body(): lax.all_gather(out_weight, ('pb', 'ka'), axis=1, tiled=True)  127 us
    all_gather x1, waiting for transfers between devices, body(): lax.all_gather(qkv_weight, ('pb', 'ka'), axis=0, tiled=True)  124 us
    unnamed x3, other arithmetic  38.5 us
    all_to_all x1, waiting for transfers between devices, gather_from_all(): lax.all_to_all(jnp.tile(shard, repeats), axis, split_axis=dim, concat_axi...  32 us
    unnamed x22, local copies, waits for them, and re-layouts  31.1 us
    another operation x1, local copies, waits for them, and re-layouts, body(): partial_value[None]  18.5 us
    dot_general x4, matrix products, attend(): jnp.einsum('hqk,khd->qhd', soft_weights.astype(jnp.bfloat16), near_values...  10.2 us
  transfers between devices with their start and end apart: 8, of which 5 were waited for; matrix products, arithmetic and copies ran while one was open for 14% of the time, Pallas kernels for 0%

profile of v1, /device:TPU:1, one launch (start us, length us, event | category | flops | bytes accessed | tf_op | source)
XLA Modules:
  0.0 487.7 jit_solution(14466848398246503076)
XLA Ops:
  10.2 124.1 %all-gather.5.cloned.1.call-done = bf16[512,2,1536]{2,1,0:T(2,128)(2,1)} async-done(((bf16[1,2,1536]{2,1,0:T(2,128)(2,1)}), bf16[512,2,1536]{2,1,0:T(2,128)(2,1)}) %all-gather.5.cloned.1.call-update) | async-done | bytes 3145744 | tf_op jit(solution)/shard_map/all_gather | solution.py:89
  134.2 6.3 %reshape.144 = bf16[1024,1536]{1,0:T(8,128)(2,1)S(1)} reshape(bf16[512,2,1536]{2,1,0:T(2,128)(2,1)} %all-gather.5.cloned.1.call-done) | data formatting | bytes 6291456
  144.8 4.4 all-to-all-start
  149.3 2.8 collective-permute-start
  152.1 5.9 %collective-permute-start.1 = (bf16[128,1024]{1,0:T(8,128)(2,1)S(1)}, bf16[128,1024]{1,0:T(8,128)(2,1)S(1)}, u32[]{:S(2)}, u32[]{:S(2)}) collective-permute-start(bf16[128,1024]{1,0:T(8,128)(2,1)S(1)} %slice.21), channel_id=1, source_target_pairs={{16,0},{32,16},{48,32},{64,48},{80,64},{96,80},{112,96},{128,112},... | collective-permute-start | bytes 786440 | tf_op jit(solution)/shard_map/ppermute | solution.py:26
  158.4 4.0 collective-permute-done
  166.2 32.0 %all-to-all-done = bf16[16,128,512]{1,2,0:T(8,128)(2,1)S(1)} async-done(((bf16[16,128,512]{1,2,0:T(8,128)(2,1)}), bf16[16,128,512]{1,2,0:T(8,128)(2,1)S(1)}, u32[]{:S(2)}, u32[]{:S(2)}) %all-to-all-start) | async-done | bytes 2097184 | tf_op jit(solution)/shard_map/all_to_all | solution.py:13
  198.2 2.7 copy.79
  200.9 2.7 reshape_reshape.7
  205.5 29.0 %while.14 = (s32[]{:T(128)}, bf16[4,512,512]{2,1,0:T(8,128)(2,1)}, bf16[4,512,8]{1,2,0:T(8,128)(2,1)S(1)}, bf16[4,512,8]{1,2,0:T(8,128)(2,1)S(1)}, pred[4,512,3]...) while((s32[]{:T(128)}, bf16[4,512,512]{2,1,0:T(8,128)(2,1)}, ...), condition=%wide.region_4.5_spmd, body=%wide.region_1.4_spmd.sunk | while | flops 420753408 | bytes 23795300 | solution.py:67
  209.1 2.5 select_convert_fusion.2
  235.7 12.2 %reduce.6 = bf16[2048,8]{1,0:T(8,128)(2,1)} reduce(bf16[2048,1,8]{2,1,0:T(2,128)(2,1)S(1)} %bitcast.103, bf16[]{:T(256)} %broadcast.130), dimensions={1}, to_apply=%bitcast.59.reduce_sub_computation | reduce | bytes 65538
  250.1 5.0 %all-to-all-start.2 = ((bf16[16,2,512]{2,1,0:T(2,128)(2,1)}), bf16[16,2,512]{2,1,0:T(2,128)(2,1)S(1)}, u32[]{:S(2)}, u32[]{:S(2)}) async-start(bf16[16,2,512]{2,1,0:T(2,128)(2,1)} %reshape.151), calls=%async_computation.2 | async-start | bytes 65536 | tf_op jit(solution)/shard_map/all_to_all | solution.py:118
  255.8 12.2 %reduce.7 = bf16[2048,8]{1,0:T(8,128)(2,1)} reduce(bf16[2048,1,8]{2,1,0:T(2,128)(2,1)S(1)} %bitcast.104, bf16[]{:T(256)} %broadcast.130), dimensions={1}, to_apply=%bitcast.57.reduce_sub_computation | reduce | bytes 65538
  270.3 7.2 %all-to-all-start.1 = ((bf16[16,2,512]{2,1,0:T(2,128)(2,1)}), bf16[16,2,512]{2,1,0:T(2,128)(2,1)S(1)}, u32[]{:S(2)}, u32[]{:S(2)}) async-start(bf16[16,2,512]{2,1,0:T(2,128)(2,1)} %reshape.149), calls=%async_computation.1 | async-start | bytes 65536 | tf_op jit(solution)/shard_map/all_to_all | solution.py:119
  277.5 18.5 %copy.99 = bf16[1,2048,512]{2,0,1:T(2,128)(2,1)} copy(bf16[1,2048,512]{2,1,0:T(8,128)(2,1)S(1)} %bitcast.107) | data formatting | bytes 4194304 | tf_op jit(solution)/shard_map/broadcast_in_dim;reshape | solution.py:117
  296.0 14.0 %reduce.5 = bf16[2048,512]{1,0:T(8,128)(2,1)S(1)} reduce(bf16[2048,1,512]{2,1,0:T(2,128)(2,1)} %bitcast.97, bf16[]{:T(256)} %broadcast.130), dimensions={1}, to_apply=%bitcast.71.reduce_sub_computation | reduce | bytes 4194306
  310.0 2.8 reshape.147
  312.8 7.2 %all-to-all-start.3 = ((bf16[16,2,32768]{2,1,0:T(2,128)(2,1)}), bf16[16,2,32768]{2,1,0:T(2,128)(2,1)S(1)}, u32[]{:S(2)}, u32[]{:S(2)}) async-start(bf16[16,2,32768]{2,1,0:T(2,128)(2,1)} %reshape.147), calls=%async_computation.3 | async-start | bytes 4194304 | tf_op jit(solution)/shard_map/all_to_all | solution.py:117
  320.8 126.8 %all-gather.7.cloned.1.call-done = bf16[512,2,512]{2,1,0:T(2,128)(2,1)} async-done(((bf16[1,2,512]{2,1,0:T(2,128)(2,1)}), bf16[512,2,512]{2,1,0:T(2,128)(2,1)}) %all-gather.7.cloned.1.call-update) | async-done | bytes 1048592 | tf_op jit(solution)/shard_map/all_gather | solution.py:132
  458.7 6.8 %reshape.148 = bf16[2048,1,512]{2,1,0:T(2,128)(2,1)} reshape(bf16[16,2,32768]{2,1,0:T(2,128)(2,1)S(1)} %all-to-all-done.3) | data formatting | bytes 4194304
  465.5 4.6 copy_convert_fusion
  470.1 5.5 %copy.92 = f32[1,2048,512]{1,2,0:T(8,128)} copy(f32[1,2048,512]{2,1,0:T(8,128)} %copy_convert_fusion) | data formatting | bytes 8388608 | tf_op jit(solution)/shard_map/convert_element_type | solution.py:121
  475.6 3.1 copy.96
  (103 shorter events, 60.4 us)
Async XLA Ops:
  6.5 1.4 copy-start
  6.5 127.7 %all-gather.5.cloned.1.call-start = ((), (), s32[]{:S(2)}) async-start(), calls=%async_computation.4 | async-start | bytes 3151872 | tf_op jit(solution)/shard_map/all_gather | solution.py:89
  142.2 0.8 copy-start.2
  142.9 15.0 %copy-start.5 = (s32[16]{0:T(128)S(1)}, s32[16]{0:T(128)}, u32[]{:S(2)}) copy-start(s32[16]{0:T(128)} %param.11) | copy-start | bytes 196
  142.9 15.1 %copy-start.4 = (s32[16,24]{1,0:T(8,128)S(1)}, s32[16,24]{1,0:T(8,128)}, u32[]{:S(2)}) copy-start(s32[16,24]{1,0:T(8,128)} %param.10) | copy-start | bytes 4612
  142.9 6.3 %copy-start.3 = (bf16[128,1536]{1,0:T(8,128)(2,1)S(1)}, bf16[128,1536]{1,0:T(8,128)(2,1)}, u32[]{:S(2)}) copy-start(bf16[128,1536]{1,0:T(8,128)(2,1)} %copy-done.2) | copy-start | bytes 1179652
  144.8 53.4 %all-to-all-start = ((bf16[16,128,512]{1,2,0:T(8,128)(2,1)}), bf16[16,128,512]{1,2,0:T(8,128)(2,1)S(1)}, u32[]{:S(2)}, u32[]{:S(2)}) async-start(bf16[16,128,512]{1,2,0:T(8,128)(2,1)} %tile.2), calls=%async_computation | async-start | bytes 4194304 | tf_op jit(solution)/shard_map/all_to_all | solution.py:13
  149.3 13.1 %collective-permute-start = (bf16[128,1024]{1,0:T(8,128)(2,1)S(1)}, bf16[128,1024]{1,0:T(8,128)(2,1)S(1)}, u32[]{:S(2)}, u32[]{:S(2)}) collective-permute-start(bf16[128,1024]{1,0:T(8,128)(2,1)S(1)} %slice.21), channel_id=1, source_target_pairs={{0,16},{16,32},{32,48},{48,64},{64,80},{80,96},{96,112},{112,128},... | collective-permute-start | bytes 786440 | tf_op jit(solution)/shard_map/ppermute | solution.py:25
  152.1 11.2 %collective-permute-start.1 = (bf16[128,1024]{1,0:T(8,128)(2,1)S(1)}, bf16[128,1024]{1,0:T(8,128)(2,1)S(1)}, u32[]{:S(2)}, u32[]{:S(2)}) collective-permute-start(bf16[128,1024]{1,0:T(8,128)(2,1)S(1)} %slice.21), channel_id=1, source_target_pairs={{16,0},{32,16},{48,32},{64,48},{80,64},{96,80},{112,96},{128,112},... | collective-permute-start | bytes 786440 | tf_op jit(solution)/shard_map/ppermute | solution.py:26
  234.5 43.0 %copy-start.1 = (bf16[4,512,512]{2,1,0:T(8,128)(2,1)S(1)}, bf16[4,512,512]{2,1,0:T(8,128)(2,1)}, u32[]{:S(2)}) copy-start(bf16[4,512,512]{2,1,0:T(8,128)(2,1)} %get-tuple-element.51) | copy-start | bytes 6291460
  250.1 20.1 %all-to-all-start.2 = ((bf16[16,2,512]{2,1,0:T(2,128)(2,1)}), bf16[16,2,512]{2,1,0:T(2,128)(2,1)S(1)}, u32[]{:S(2)}, u32[]{:S(2)}) async-start(bf16[16,2,512]{2,1,0:T(2,128)(2,1)} %reshape.151), calls=%async_computation.2 | async-start | bytes 65536 | tf_op jit(solution)/shard_map/all_to_all | solution.py:118
  270.3 42.6 %all-to-all-start.1 = ((bf16[16,2,512]{2,1,0:T(2,128)(2,1)}), bf16[16,2,512]{2,1,0:T(2,128)(2,1)S(1)}, u32[]{:S(2)}, u32[]{:S(2)}) async-start(bf16[16,2,512]{2,1,0:T(2,128)(2,1)} %reshape.149), calls=%async_computation.1 | async-start | bytes 65536 | tf_op jit(solution)/shard_map/all_to_all | solution.py:119
  312.8 145.8 %all-to-all-start.3 = ((bf16[16,2,32768]{2,1,0:T(2,128)(2,1)}), bf16[16,2,32768]{2,1,0:T(2,128)(2,1)S(1)}, u32[]{:S(2)}, u32[]{:S(2)}) async-start(bf16[16,2,32768]{2,1,0:T(2,128)(2,1)} %reshape.147), calls=%async_computation.3 | async-start | bytes 4194304 | tf_op jit(solution)/shard_map/all_to_all | solution.py:117
  320.1 127.6 %all-gather.7.cloned.1.call-start = ((), (), s32[]{:S(2)}) async-start(), calls=%async_computation.5 | async-start | bytes 1050624 | tf_op jit(solution)/shard_map/all_gather | solution.py:132
Sparse Core Ops, SparseCore 0:
  11.5 122.6 all-gather.4
  325.1 122.5 all-gather.6
